TPU v7x, 32 devices: a whole 2x2x4 slice. The times are simulated.
32 devices in a mesh: groups: 2 (over y), tensor: 16 (over z, x, core).
Axes of the slice: x: 2, y: 2, z: 4, core: 2. Of those that a mesh axis runs over, the one named last changes fastest.
Arguments:
- token_ids: int32 [16, 4], P('tensor', 'groups'), parts along dimension 1, may hold values from 0 to 63
- lengths: int32 [4], P('groups'), parts along dimension 0, may hold values from 8 to 16, as said below
- embed_table: bfloat16 [64, 6144], replicated, may hold values from -6 to 6
- gain_attn: float32 [6144], replicated, may hold values from 0.1 to 1.9
- w_qkv: bfloat16 [6144, 18432], P(None, 'tensor'), may hold values from -0.078125 to 0.078125
- w_out: bfloat16 [6144, 6144], P(None, 'tensor'), may hold values from -0.078125 to 0.078125
- gain_first: float32 [6144], replicated, may hold values from 0.1 to 1.9
- gate_first: bfloat16 [6144, 16384], P(None, 'tensor'), may hold values from -0.078125 to 0.078125
- up_first: bfloat16 [6144, 16384], P(None, 'tensor'), may hold values from -0.078125 to 0.078125
- down_first: bfloat16 [16384, 6144], P('tensor'), may hold values from -0.09375 to 0.09375
- gain_second: float32 [6144], replicated, may hold values from 0.1 to 1.9
- gate_second: bfloat16 [6144, 16384], P(None, 'tensor'), may hold values from -0.078125 to 0.078125
- up_second: bfloat16 [6144, 16384], P(None, 'tensor'), may hold values from -0.078125 to 0.078125
- down_second: bfloat16 [16384, 6144], P('tensor'), may hold values from -0.09375 to 0.09375
Outputs:
- states: bfloat16 [16, 4, 6144], P('tensor', 'groups'), parts along dimension 1
There are 2 independent parts, one for each index of `groups`. A program takes and returns all parts, laid end to end along the dimension named above; an argument that names none is the same for every part. Nothing has to cross between parts.
Inputs may be any that keep to these rules, and one draw needn't show every extreme that they name: `lengths`: each micro-batch holds one protein of at least half of 16 positions; in every draw one micro-batch is full, 16 positions.
All inputs are finite; a program needn't handle non-finite values.
Results may differ from a plain program's by a relative error of at most 0.013.
Values may be sent and summed in bfloat16 or wider, within the bound.
No kernel may reach another device: no remote copies, remote signals or barrier semaphores. Data moves between devices by JAX's collectives and lax.ppermute only.
A program may use at most 192 MiB of HBM per device.

v0:
```python
import jax
import jax.numpy as jnp
from jax import lax
from jax.sharding import PartitionSpec as P

H = 48
HD = 128


def norm_rows(values, gain_vec):
    row_mean = jnp.mean(values, axis=-1, keepdims=True)
    centred = values - row_mean
    row_var = jnp.mean(centred * centred, axis=-1, keepdims=True)
    return (centred * lax.rsqrt(row_var + 1e-05) * gain_vec).astype(jnp.bfloat16)


def local_hidden(normed, gate_mat, up_mat):
    gated = jnp.einsum("pmd,dc->pmc", normed, gate_mat, preferred_element_type=jnp.float32)
    lifted = jnp.einsum("pmd,dc->pmc", normed, up_mat, preferred_element_type=jnp.float32)
    return (jax.nn.silu(gated) * lifted).astype(jnp.bfloat16)


def spread_rows(local_rows, row_fn):
    return row_fn(lax.all_gather(local_rows, "tensor", axis=0, tiled=True), jnp.int32(0))


def to_tokens(columns):
    return lax.all_to_all(columns, "tensor", split_axis=0, concat_axis=2, tiled=True)


def down_sum(hidden_all, down_mat):
    return lax.psum_scatter(
        jnp.einsum("pmc,cd->pmd", hidden_all, down_mat, preferred_element_type=jnp.float32),
        "tensor",
        scatter_dimension=0,
        tiled=True,
    )


def local(
    token_ids,
    lengths,
    embed_table,
    gain_attn,
    w_qkv,
    w_out,
    gain_first,
    gate_first,
    up_first,
    down_first,
    gain_second,
    gate_second,
    up_second,
    down_second,
):
    rows_here = token_ids.shape[0]
    micro_count = token_ids.shape[1]
    vocab_size = embed_table.shape[0]
    own_start = lax.axis_index("tensor") * rows_here
    onehot = (token_ids[:, :, None] == jnp.arange(vocab_size)[None, None, :]).astype(jnp.bfloat16)
    embedded = jnp.einsum("pmv,vd->pmd", onehot, embed_table, preferred_element_type=jnp.float32)
    normed_attn = norm_rows(embedded, gain_attn)

    def qkv_rows(row_piece, row_start):
        return jnp.einsum(
            "pmd,dc->pmc", row_piece, w_qkv, preferred_element_type=jnp.float32
        ).astype(jnp.bfloat16)

    projected = to_tokens(spread_rows(normed_attn, qkv_rows))
    feat_width = projected.shape[2] // 3
    queries = projected[..., :feat_width].reshape(rows_here, micro_count, H, HD)
    key_rows = projected[..., feat_width : 2 * feat_width]
    value_rows = projected[..., 2 * feat_width :]
    score_scale = HD ** (-0.5)
    key_piece = lax.all_gather(key_rows, "tensor", axis=0, tiled=True)
    value_piece = lax.all_gather(value_rows, "tensor", axis=0, tiled=True)
    piece_rows = key_piece.shape[0]
    key_heads = key_piece.reshape(piece_rows, micro_count, H, HD)
    value_heads = value_piece.reshape(piece_rows, micro_count, H, HD)
    scores = (
        jnp.einsum("pmhe,qmhe->pmhq", queries, key_heads, preferred_element_type=jnp.float32)
        * score_scale
    )
    positions = jnp.arange(piece_rows)
    live_keys = (positions[None, :] < lengths[:, None]).astype(jnp.float32)
    weights = jnp.exp(scores) * live_keys[None, :, None, :]
    denominator = jnp.sum(weights, axis=-1)
    numerator = jnp.einsum(
        "pmhq,qmhe->pmhe",
        weights.astype(jnp.bfloat16),
        value_heads,
        preferred_element_type=jnp.float32,
    )
    numerator, denominator = (numerator, denominator)
    attended = (
        (numerator / denominator[..., None])
        .reshape(rows_here, micro_count, feat_width)
        .astype(jnp.bfloat16)
    )

    def out_rows(row_piece, row_start):
        return jnp.einsum(
            "pmd,dc->pmc", row_piece, w_out, preferred_element_type=jnp.float32
        ).astype(jnp.bfloat16)

    after_attn = embedded + to_tokens(spread_rows(attended, out_rows)).astype(jnp.float32)

    def first_rows(row_piece, row_start):
        return local_hidden(row_piece, gate_first, up_first)

    hidden_first = spread_rows(norm_rows(after_attn, gain_first), first_rows)
    partial_all = jnp.einsum(
        "pmc,cd->pmd", hidden_first, down_first, preferred_element_type=jnp.float32
    )
    own_rows = lax.dynamic_slice_in_dim(partial_all, own_start, rows_here, 0) + after_attn
    partial_all = lax.dynamic_update_slice_in_dim(partial_all, own_rows, own_start, 0)
    first_all = lax.psum(partial_all, "tensor")
    after_first = lax.dynamic_slice_in_dim(first_all, own_start, rows_here, 0)
    hidden_second = local_hidden(norm_rows(first_all, gain_second), gate_second, up_second)
    after_second = after_first + down_sum(hidden_second, down_second)
    return after_second.astype(jnp.bfloat16)


def solution(mesh):
    return jax.shard_map(
        local,
        mesh=mesh,
        in_specs=(
            P("tensor", "groups"),
            P("groups"),
            P(),
            P(),
            P(None, "tensor"),
            P(None, "tensor"),
            P(),
            P(None, "tensor"),
            P(None, "tensor"),
            P("tensor", None),
            P(),
            P(None, "tensor"),
            P(None, "tensor"),
            P("tensor", None),
        ),
        out_specs=P("tensor", "groups", None),
        check_vma=False,
    )
```

profile of v0, /device:TPU:0, one launch (start us, length us, event | category | flops | bytes accessed | tf_op | source)
XLA Modules:
  0.0 383.6 jit_solution(4767694113768598177)
XLA Ops:
  6.5 1.1 copy-done
  7.7 1.0 fusion.79
  9.0 0.8 fusion.64
  9.8 24.2 %all-gather.2 = bf16[16,2,6144]{2,1,0:T(2,128)(2,1)S(1)} all-gather(bf16[1,2,6144]{2,1,0:T(2,128)(2,1)S(1)} %fusion.64), channel_id=2, replica_groups=mesh['groups'=2,'tensor'=16] {'tensor'}, dimensions={0}, use_global_device_ids=true | all-gather | bytes 417792 | tf_op jit(solution)/shard_map/all_gather | solution.py:24
  34.0 7.6 %fusion.16 = bf16[16,2,1152]{2,0,1:T(8,128)(2,1)S(1)} fusion(bf16[6144,1152]{1,0:T(8,128)(2,1)} %param.18, bf16[16,2,6144]{2,1,0:T(2,128)(2,1)S(1)} %all-gather.2), kind=kOutput, calls=%fused_computation.16 | convolution fusion | flops 453021696 | bytes 14622720 | tf_op jit(solution)/shard_map/pmd,dc->pmc/dot_general | solution.py:65
  41.6 0.7 copy.49
  42.2 3.5 all-to-all-start
  45.8 6.9 %all-to-all-done = bf16[16,2,1152]{2,1,0:T(2,128)(2,1)S(1)} async-done(((bf16[16,2,1152]{2,1,0:T(2,128)(2,1)}), bf16[16,2,1152]{2,1,0:T(2,128)(2,1)S(1)}, u32[]{:S(2)}, u32[]{:S(2)}) %all-to-all-start) | async-done | bytes 73760 | tf_op jit(solution)/shard_map/all_to_all | solution.py:28
  52.8 18.8 %all_gather.17 = bf16[16,2,6144]{2,1,0:T(2,128)(2,1)S(1)} all-gather(bf16[1,2,6144]{2,1,0:T(2,128)(2,1)S(1)} %get-tuple-element.9), channel_id=1, replica_groups=mesh['groups'=2,'tensor'=16] {'tensor'}, dimensions={0}, use_global_device_ids=true | all-gather | bytes 417792 | tf_op jit(solution)/shard_map/all_gather | solution.py:75
  71.6 0.2 reshape.163
  71.8 0.3 fusion.40
  72.4 19.6 %all_gather.16 = bf16[16,2,6144]{2,1,0:T(2,128)(2,1)S(1)} all-gather(bf16[1,2,6144]{2,1,0:T(2,128)(2,1)S(1)} %get-tuple-element.7), channel_id=1, replica_groups=mesh['groups'=2,'tensor'=16] {'tensor'}, dimensions={0}, use_global_device_ids=true | all-gather | bytes 417792 | tf_op jit(solution)/shard_map/all_gather | solution.py:76
  92.7 19.0 %all_gather.18 = bf16[16,2,6144]{2,1,0:T(2,128)(2,1)S(1)} all-gather(bf16[1,2,6144]{2,1,0:T(2,128)(2,1)S(1)} %convert_element_type.75), channel_id=1, replica_groups=mesh['groups'=2,'tensor'=16] {'tensor'}, dimensions={0}, use_global_device_ids=true | all-gather | bytes 417792 | tf_op jit(solution)/shard_map/all_gather | solution.py:24
  111.6 3.1 fusion.35
  114.8 0.6 copy.51
  115.4 3.5 all-to-all-start.1
  119.0 6.5 %all-to-all-done.1 = bf16[16,2,384]{2,1,0:T(2,128)(2,1)S(1)} async-done(((bf16[16,2,384]{2,1,0:T(2,128)(2,1)}), bf16[16,2,384]{2,1,0:T(2,128)(2,1)S(1)}, u32[]{:S(2)}, u32[]{:S(2)}) %all-to-all-start.1) | async-done | bytes 24608 | tf_op jit(solution)/shard_map/all_to_all | solution.py:28
  126.0 18.6 %all-gather.3 = bf16[16,2,6144]{2,1,0:T(2,128)(2,1)S(1)} all-gather(bf16[1,2,6144]{2,1,0:T(2,128)(2,1)S(1)} %fusion.65), channel_id=3, replica_groups=mesh['groups'=2,'tensor'=16] {'tensor'}, dimensions={0}, use_global_device_ids=true | all-gather | bytes 417792 | tf_op jit(solution)/shard_map/all_gather | solution.py:24
  144.7 6.8 %fusion.12 = f32[16,2,1024]{2,0,1:T(8,128)S(1)} fusion(bf16[6144,1024]{1,0:T(8,128)(2,1)} %param.21, bf16[16,2,6144]{2,1,0:T(2,128)(2,1)S(1)} %all-gather.3), kind=kOutput, calls=%fused_computation.12 | convolution fusion | flops 402653184 | bytes 13107200 | tf_op jit(solution)/shard_map/pmd,dc->pmc/dot_general | solution.py:18
  151.5 12.6 %fusion.8 = f32[16,2,6144]{2,0,1:T(8,128)S(1)} fusion(bf16[1024,6144]{1,0:T(8,128)(2,1)} %param.23, bf16[6144,1024]{1,0:T(8,128)(2,1)} %param.22, bf16[16,2,6144]{2,1,0:T(2,128)(2,1)S(1)} %all-gather.3, f32[16,2,1024]{2,0,1:T(8,128)S(1)} %fusion.12), kind=kOutput, calls=%fused_computation.8 | convolution fusion | flops 805502976 | bytes 26476544 | tf_op jit(solution)/shard_map/pmc,cd->pmd/dot_general | solution.py:112
  164.1 0.6 copy.55
  164.8 0.9 copy-done.2
  165.9 91.0 %all-reduce.4.cloned.1.call-done = f32[16,2,6144]{2,1,0:T(2,128)} async-done(((f32[16,2,6144]{2,1,0:T(2,128)}), f32[16,2,6144]{2,1,0:T(2,128)}) %all-reduce.4.cloned.1.call-update) | async-done | bytes 786448 | tf_op jit(solution)/shard_map/psum | solution.py:117
  256.9 1.4 reduce_sum.68
  258.4 1.7 multiply_reduce_fusion
  260.1 1.7 multiply_convert_fusion
  261.7 6.9 %fusion.6 = f32[16,2,1024]{2,0,1:T(8,128)S(1)} fusion(bf16[6144,1024]{1,0:T(8,128)(2,1)} %param.25, bf16[16,2,6144]{2,1,0:T(2,128)(2,1)S(1)} %multiply_convert_fusion), kind=kOutput, calls=%fused_computation.6 | convolution fusion | flops 402653184 | bytes 13107200 | tf_op jit(solution)/shard_map/pmd,dc->pmc/dot_general | solution.py:18
  268.7 12.6 %fusion.2 = f32[16,2,6144]{2,0,1:T(8,128)S(1)} fusion(bf16[1024,6144]{1,0:T(8,128)(2,1)} %param.27, bf16[6144,1024]{1,0:T(8,128)(2,1)} %param.26, bf16[16,2,6144]{2,1,0:T(2,128)(2,1)S(1)} %multiply_convert_fusion, f32[16,2,1024]{2,0,1:T(8,128)S(1)} %fusion.6), kind=kOutput, calls=%fused_computation.2 | convolution fusion | flops 805502976 | bytes 26476544 | tf_op jit(solution)/shard_map/pmc,cd->pmd/dot_general | solution.py:33
  281.3 1.5 copy.58
  282.8 0.6 dynamic-slice
  283.4 91.3 %all-reduce.6.cloned.1.call-done = f32[16,2,6144]{2,1,0:T(2,128)} async-done(((f32[16,2,6144]{2,1,0:T(2,128)}), f32[16,2,6144]{2,1,0:T(2,128)}) %all-reduce.6.cloned.1.call-update) | async-done | bytes 786448
  374.7 2.0 fusion.62
  (38 shorter events, 2.2 us)
Async XLA Ops:
  6.5 1.1 copy-start
  6.5 39.2 %copy-start.5 = (s32[2]{0:T(128)S(1)}, s32[2]{0:T(128)}, u32[]{:S(2)}) copy-start(s32[2]{0:T(128)} %param.15) | copy-start | bytes 28
  34.0 91.9 %copy-start.3 = (f32[6144]{0:T(1024)S(1)}, f32[6144]{0:T(1024)}, u32[]{:S(2)}) copy-start(f32[6144]{0:T(1024)} %param.20) | copy-start | bytes 73732
  42.2 10.5 %all-to-all-start = ((bf16[16,2,1152]{2,1,0:T(2,128)(2,1)}), bf16[16,2,1152]{2,1,0:T(2,128)(2,1)S(1)}, u32[]{:S(2)}, u32[]{:S(2)}) async-start(bf16[16,2,1152]{2,1,0:T(2,128)(2,1)} %copy.49), calls=%async_computation | async-start | bytes 147456 | tf_op jit(solution)/shard_map/all_to_all | solution.py:28
  115.4 10.0 %all-to-all-start.1 = ((bf16[16,2,384]{2,1,0:T(2,128)(2,1)}), bf16[16,2,384]{2,1,0:T(2,128)(2,1)S(1)}, u32[]{:S(2)}, u32[]{:S(2)}) async-start(bf16[16,2,384]{2,1,0:T(2,128)(2,1)} %copy.51), calls=%async_computation.1 | async-start | bytes 49152 | tf_op jit(solution)/shard_map/all_to_all | solution.py:28
  118.9 138.0 %all-reduce.4.cloned.1.call-start = ((), (), s32[]{:S(2)}) async-start(), calls=%async_computation.2 | async-start | bytes 1572864 | tf_op jit(solution)/shard_map/psum | solution.py:117
  151.5 108.6 %copy-start.4 = (f32[6144]{0:T(1024)S(1)}, f32[6144]{0:T(1024)}, u32[]{:S(2)}) copy-start(f32[6144]{0:T(1024)} %param.24) | copy-start | bytes 73732
  164.8 0.9 copy-start.2
  165.7 209.0 %all-reduce.6.cloned.1.call-start = ((), (), s32[]{:S(2)}) async-start(), calls=%async_computation.3 | async-start | bytes 1572864
  261.7 115.0 %copy-start.1 = (bf16[64,6144]{1,0:T(8,128)(2,1)S(1)}, bf16[64,6144]{1,0:T(8,128)(2,1)}, u32[]{:S(2)}) copy-start(bf16[64,6144]{1,0:T(8,128)(2,1)} %param.16) | copy-start | bytes 2359300
  268.7 14.2 %copy-start.6 = (u32[32]{0:T(128)S(1)}, u32[32]{0:T(128)}, u32[]{:S(2)}) copy-start(u32[32]{0:T(128)} %constant.31) | copy-start | bytes 388
Sparse Core Ops, SparseCore 0:
  165.8 91.0 all-reduce.3
  282.9 91.7 all-reduce.5
where the time goes:
time: 384 us
  waiting for transfers between devices  196 us (51%)
  blocking collectives  100 us (26%)
  matrix products  51.3 us (13%)
  between operations  13.6 us (4%)
  other arithmetic  8.77 us (2%)
  starting transfers between devices  7.26 us (2%)
  local copies, waits for them, and re-layouts  6.84 us (2%)
    unnamed x3, waiting for transfers between devices  91.3 us
    psum x1, waiting for transfers between devices, local(): first_all = lax.psum(partial_all, 'tensor')  91 us
    all_gather x3, blocking collectives, spread_rows(): lax.all_gather(local_rows, 'tensor', axis=0, tiled=True)  61.8 us
    all_gather x1, blocking collectives, local(): value_piece = lax.all_gather(value_rows, 'tensor', axis=0, tiled=True)  19.6 us
    all_gather x1, blocking collectives, local(): key_piece = lax.all_gather(key_rows, 'tensor', axis=0, tiled=True)  18.8 us
    dot_general x2, matrix products, local_hidden(): jnp.einsum('pmd,dc->pmc', normed, gate_mat, preferred_element_type=jnp.fl...  13.7 us
    all_to_all x2, waiting for transfers between devices, to_tokens(): lax.all_to_all(columns, 'tensor', split_axis=0, concat_axis=2, tiled=True)  13.3 us
    dot_general x1, matrix products, down_sum(): jnp.einsum('pmc,cd->pmd', hidden_all, down_mat, preferred_element_type=jn...  12.6 us
  transfers between devices with their start and end apart: 4, of which 4 were waited for; matrix products, arithmetic and copies ran while one was open for 0% of the time, Pallas kernels for 0%

commit v1 on v0

--- a/solution.py
+++ b/solution.py
@@ -1,3 +1,4 @@
+import functools
 import jax
 import jax.numpy as jnp
 from jax import lax
@@ -5,6 +6,36 @@
 
 H = 48
 HD = 128
+
+
+def solve_the_desk(target, pos_dim):
+    t_next = lax.axis_size("tensor")
+    z2 = lax.axis_index("tensor")
+    p_next, carry_out, after = (t_next, z2, target.shape[pos_dim])
+    stack_in = [(hop_no, (hop_no + 1) % p_next) for hop_no in range(p_next)]
+    found = [(hop_no, (hop_no - 1) % p_next) for hop_no in range(p_next)]
+    z = jnp.zeros(
+        (*target.shape[:pos_dim], p_next * after, *target.shape[pos_dim + 1 :]), target.dtype
+    )
+    z = lax.dynamic_update_slice_in_dim(z, target, carry_out * after, axis=pos_dim)
+    odd = p_next // 2
+    i = 1
+    small = z_new = target
+    while i < odd + 1:
+        small = lax.ppermute(small, axis_name="tensor", perm=stack_in)
+        z = lax.dynamic_update_slice_in_dim(
+            z, small, (carry_out - i) % p_next * after, axis=pos_dim
+        )
+        if i < p_next - odd:
+            z_new = lax.ppermute(z_new, axis_name="tensor", perm=found)
+            z = lax.dynamic_update_slice_in_dim(
+                z, z_new, (carry_out + i) % p_next * after, axis=pos_dim
+            )
+        i = i + 1
+    return z
+
+
+blocks_step_on = functools.partial(solve_the_desk, pos_dim=0)
 
 
 def norm_rows(values, gain_vec):
@@ -73,7 +104,7 @@
     value_rows = projected[..., 2 * feat_width :]
     score_scale = HD ** (-0.5)
     key_piece = lax.all_gather(key_rows, "tensor", axis=0, tiled=True)
-    value_piece = lax.all_gather(value_rows, "tensor", axis=0, tiled=True)
+    value_piece = blocks_step_on(value_rows)
     piece_rows = key_piece.shape[0]
     key_heads = key_piece.reshape(piece_rows, micro_count, H, HD)
     value_heads = value_piece.reshape(piece_rows, micro_count, H, HD)

time: 384 us -> 409 us (1.065)
  starting transfers between devices: 7.26 us -> 34.9 us
  blocking collectives: 100 us -> 89.4 us
  waiting for transfers between devices: 196 us -> 203 us
    ppermute x0 -> x15, starting transfers between devices: none -> 31.1 us  [the longest x7 30.7 us: solve_the_desk(): z_new = lax.ppermute(z_new, axis_name='tensor', perm=found)]
    all_gather x1 -> x0, blocking collectives: 19.6 us -> none  [local(): value_piece = lax.all_gather(value_rows, 'tensor', axis=0, tiled=True)]
    ppermute x0 -> x15, waiting for transfers between devices: none -> 14.6 us  [the longest x8 14.5 us: solve_the_desk(): small = lax.ppermute(small, axis_name='tensor', perm=stack_in)]
    all_to_all x0 -> x1, blocking collectives: none -> 9.95 us  [to_tokens(): lax.all_to_all(columns, 'tensor', split_axis=0, concat_axis=2, tiled=True)]
    all_to_all x2 -> x1, waiting for transfers between devices: 13.3 us -> 6.52 us  [to_tokens(): lax.all_to_all(columns, 'tensor', split_axis=0, concat_axis=2, tiled=True)]
  transfers between devices with their start and end apart: 4 -> 18, of which waited for: 4 -> 10; matrix products, arithmetic and copies ran while one was open for 0% -> 0% of each run, Pallas kernels for 0% -> 0%
where the time goes in v1:
time: 409 us
  waiting for transfers between devices  203 us (50%)
  blocking collectives  89.4 us (22%)
  matrix products  51.3 us (13%)
  starting transfers between devices  34.9 us (9%)
  between operations  13.9 us (3%)
  other arithmetic  8.84 us (2%)
  local copies, waits for them, and re-layouts  6.96 us (2%)
    unnamed x3, waiting for transfers between devices  91.3 us
    psum x1, waiting for transfers between devices, local(): first_all = lax.psum(partial_all, 'tensor')  90.9 us
    all_gather x3, blocking collectives, spread_rows(): lax.all_gather(local_rows, 'tensor', axis=0, tiled=True)  61.2 us
    ppermute x7, starting transfers between devices, solve_the_desk(): z_new = lax.ppermute(z_new, axis_name='tensor', perm=found)  30.7 us
    all_gather x1, blocking collectives, local(): key_piece = lax.all_gather(key_rows, 'tensor', axis=0, tiled=True)  18.2 us
    ppermute x8, waiting for transfers between devices, solve_the_desk(): small = lax.ppermute(small, axis_name='tensor', perm=stack_in)  14.5 us
    dot_general x2, matrix products, local_hidden(): jnp.einsum('pmd,dc->pmc', normed, gate_mat, preferred_element_type=jnp.fl...  13.7 us
    dot_general x1, matrix products, down_sum(): jnp.einsum('pmc,cd->pmd', hidden_all, down_mat, preferred_element_type=jn...  12.6 us
  transfers between devices with their start and end apart: 18, of which 10 were waited for; matrix products, arithmetic and copies ran while one was open for 0% of the time, Pallas kernels for 0%

profile of v1, /device:TPU:0, one launch (start us, length us, event | category | flops | bytes accessed | tf_op | source)
XLA Modules:
  0.0 408.6 jit_solution(6879594087325261260)
XLA Ops:
  9.8 24.2 %all-gather.2 = bf16[16,2,6144]{2,1,0:T(2,128)(2,1)S(1)} all-gather(bf16[1,2,6144]{2,1,0:T(2,128)(2,1)S(1)} %fusion.64), channel_id=2, replica_groups=mesh['groups'=2,'tensor'=16] {'tensor'}, dimensions={0}, use_global_device_ids=true | all-gather | bytes 417792 | tf_op jit(solution)/shard_map/all_gather | solution.py:55
  34.0 7.6 %fusion.16 = bf16[16,2,1152]{2,0,1:T(8,128)(2,1)S(1)} fusion(bf16[6144,1152]{1,0:T(8,128)(2,1)} %param.18, bf16[16,2,6144]{2,1,0:T(2,128)(2,1)S(1)} %all-gather.2), kind=kOutput, calls=%fused_computation.16 | convolution fusion | flops 453021696 | bytes 14622720 | tf_op jit(solution)/shard_map/pmd,dc->pmc/dot_general | solution.py:96
  42.2 3.5 all-to-all-start
  46.2 6.5 %all-to-all-done = bf16[16,2,1152]{2,1,0:T(2,128)(2,1)S(1)} async-done(((bf16[16,2,1152]{2,1,0:T(2,128)(2,1)}), bf16[16,2,1152]{2,1,0:T(2,128)(2,1)S(1)}, u32[]{:S(2)}, u32[]{:S(2)}) %all-to-all-start) | async-done | bytes 73760 | tf_op jit(solution)/shard_map/all_to_all | solution.py:59
  53.0 4.4 %collective-permute-start.1 = (bf16[1,2,6144]{2,1,0:T(2,128)(2,1)S(1)}, bf16[1,2,6144]{2,1,0:T(2,128)(2,1)S(1)}, u32[]{:S(2)}, u32[]{:S(2)}) collective-permute-start(bf16[1,2,6144]{2,1,0:T(2,128)(2,1)S(1)} %get-tuple-element.7), channel_id=1, source_target_pairs={{0,15},{1,0},{2,1},{3,2},{4,3},{5,4},{6,5},{7,6},{8,7},{9,8},{10,9... | collective-permute-start | bytes 73736 | tf_op jit(solution)/shard_map/ppermute | solution.py:30
  57.5 18.2 %all_gather.13 = bf16[16,2,6144]{2,1,0:T(2,128)(2,1)S(1)} all-gather(bf16[1,2,6144]{2,1,0:T(2,128)(2,1)S(1)} %get-tuple-element.10), channel_id=1, replica_groups=mesh['groups'=2,'tensor'=16] {'tensor'}, dimensions={0}, use_global_device_ids=true | all-gather | bytes 417792 | tf_op jit(solution)/shard_map/all_gather | solution.py:106
  77.0 4.1 %collective-permute-start.3 = (bf16[1,2,6144]{2,1,0:T(2,128)(2,1)S(1)}, bf16[1,2,6144]{2,1,0:T(2,128)(2,1)S(1)}, u32[]{:S(2)}, u32[]{:S(2)}) collective-permute-start(bf16[1,2,6144]{2,1,0:T(2,128)(2,1)S(1)} %collective-permute-done.1), channel_id=1, source_target_pairs={{0,15},{1,0},{2,1},{3,2},{4,3},{5,4},{6,5},{7,6},{8,7},{9,8},{10,9... | collective-permute-start | bytes 73736 | tf_op jit(solution)/shard_map/ppermute | solution.py:30
  81.2 1.4 collective-permute-done.2
  82.6 4.4 %collective-permute-start.5 = (bf16[1,2,6144]{2,1,0:T(2,128)(2,1)S(1)}, bf16[1,2,6144]{2,1,0:T(2,128)(2,1)S(1)}, u32[]{:S(2)}, u32[]{:S(2)}) collective-permute-start(bf16[1,2,6144]{2,1,0:T(2,128)(2,1)S(1)} %collective-permute-done.3), channel_id=1, source_target_pairs={{0,15},{1,0},{2,1},{3,2},{4,3},{5,4},{6,5},{7,6},{8,7},{9,8},{10,9... | collective-permute-start | bytes 73736 | tf_op jit(solution)/shard_map/ppermute | solution.py:30
  87.1 1.4 collective-permute-done.4
  88.6 4.4 %collective-permute-start.7 = (bf16[1,2,6144]{2,1,0:T(2,128)(2,1)S(1)}, bf16[1,2,6144]{2,1,0:T(2,128)(2,1)S(1)}, u32[]{:S(2)}, u32[]{:S(2)}) collective-permute-start(bf16[1,2,6144]{2,1,0:T(2,128)(2,1)S(1)} %collective-permute-done.5), channel_id=1, source_target_pairs={{0,15},{1,0},{2,1},{3,2},{4,3},{5,4},{6,5},{7,6},{8,7},{9,8},{10,9... | collective-permute-start | bytes 73736 | tf_op jit(solution)/shard_map/ppermute | solution.py:30
  93.1 1.4 collective-permute-done.6
  94.5 4.4 %collective-permute-start.9 = (bf16[1,2,6144]{2,1,0:T(2,128)(2,1)S(1)}, bf16[1,2,6144]{2,1,0:T(2,128)(2,1)S(1)}, u32[]{:S(2)}, u32[]{:S(2)}) collective-permute-start(bf16[1,2,6144]{2,1,0:T(2,128)(2,1)S(1)} %collective-permute-done.7), channel_id=1, source_target_pairs={{0,15},{1,0},{2,1},{3,2},{4,3},{5,4},{6,5},{7,6},{8,7},{9,8},{10,9... | collective-permute-start | bytes 73736 | tf_op jit(solution)/shard_map/ppermute | solution.py:30
  99.0 1.4 collective-permute-done.8
  100.5 4.4 %collective-permute-start.11 = (bf16[1,2,6144]{2,1,0:T(2,128)(2,1)S(1)}, bf16[1,2,6144]{2,1,0:T(2,128)(2,1)S(1)}, u32[]{:S(2)}, u32[]{:S(2)}) collective-permute-start(bf16[1,2,6144]{2,1,0:T(2,128)(2,1)S(1)} %collective-permute-done.9), channel_id=1, source_target_pairs={{0,15},{1,0},{2,1},{3,2},{4,3},{5,4},{6,5},{7,6},{8,7},{9,8},{10,9... | collective-permute-start | bytes 73736 | tf_op jit(solution)/shard_map/ppermute | solution.py:30
  105.0 1.4 collective-permute-done.10
  106.4 4.4 %collective-permute-start.13 = (bf16[1,2,6144]{2,1,0:T(2,128)(2,1)S(1)}, bf16[1,2,6144]{2,1,0:T(2,128)(2,1)S(1)}, u32[]{:S(2)}, u32[]{:S(2)}) collective-permute-start(bf16[1,2,6144]{2,1,0:T(2,128)(2,1)S(1)} %collective-permute-done.11), channel_id=1, source_target_pairs={{0,15},{1,0},{2,1},{3,2},{4,3},{5,4},{6,5},{7,6},{8,7},{9,8},{10,9... | collective-permute-start | bytes 73736 | tf_op jit(solution)/shard_map/ppermute | solution.py:30
  112.4 5.9 %collective-permute-done.14 = bf16[1,2,6144]{2,1,0:T(2,128)(2,1)S(1)} collective-permute-done((bf16[1,2,6144]{2,1,0:T(2,128)(2,1)S(1)}, bf16[1,2,6144]{2,1,0:T(2,128)(2,1)S(1)}, u32[]{:S(2)}, u32[]{:S(2)}) %collective-permute-start.14) | collective-permute-done | bytes 24608 | tf_op jit(solution)/shard_map/ppermute | solution.py:25
  119.0 18.3 %all_gather.14 = bf16[16,2,6144]{2,1,0:T(2,128)(2,1)S(1)} all-gather(bf16[1,2,6144]{2,1,0:T(2,128)(2,1)S(1)} %convert_element_type.75), channel_id=1, replica_groups=mesh['groups'=2,'tensor'=16] {'tensor'}, dimensions={0}, use_global_device_ids=true | all-gather | bytes 417792 | tf_op jit(solution)/shard_map/all_gather | solution.py:55
  137.2 3.1 fusion.35
  140.4 10.0 %all_to_all.27 = bf16[16,2,384]{2,1,0:T(2,128)(2,1)S(1)} all-to-all(bf16[16,2,384]{2,1,0:T(2,128)(2,1)S(1)} %copy.51), channel_id=1, replica_groups=mesh['groups'=2,'tensor'=16] {'tensor'}, dimensions={0} | all-to-all | bytes 49152 | tf_op jit(solution)/shard_map/all_to_all | solution.py:59
  150.9 18.8 %all-gather.3 = bf16[16,2,6144]{2,1,0:T(2,128)(2,1)S(1)} all-gather(bf16[1,2,6144]{2,1,0:T(2,128)(2,1)S(1)} %fusion.65), channel_id=3, replica_groups=mesh['groups'=2,'tensor'=16] {'tensor'}, dimensions={0}, use_global_device_ids=true | all-gather | bytes 417792 | tf_op jit(solution)/shard_map/all_gather | solution.py:55
  169.7 6.8 %fusion.12 = f32[16,2,1024]{2,0,1:T(8,128)S(1)} fusion(bf16[6144,1024]{1,0:T(8,128)(2,1)} %param.21, bf16[16,2,6144]{2,1,0:T(2,128)(2,1)S(1)} %all-gather.3), kind=kOutput, calls=%fused_computation.12 | convolution fusion | flops 402653184 | bytes 13107200 | tf_op jit(solution)/shard_map/pmd,dc->pmc/dot_general | solution.py:49
  176.6 12.6 %fusion.8 = f32[16,2,6144]{2,0,1:T(8,128)S(1)} fusion(bf16[1024,6144]{1,0:T(8,128)(2,1)} %param.23, bf16[6144,1024]{1,0:T(8,128)(2,1)} %param.22, bf16[16,2,6144]{2,1,0:T(2,128)(2,1)S(1)} %all-gather.3, f32[16,2,1024]{2,0,1:T(8,128)S(1)} %fusion.12), kind=kOutput, calls=%fused_computation.8 | convolution fusion | flops 805502976 | bytes 26476544 | tf_op jit(solution)/shard_map/pmc,cd->pmd/dot_general | solution.py:143
  191.1 90.9 %all-reduce.4.cloned.1.call-done = f32[16,2,6144]{2,1,0:T(2,128)} async-done(((f32[16,2,6144]{2,1,0:T(2,128)}), f32[16,2,6144]{2,1,0:T(2,128)}) %all-reduce.4.cloned.1.call-update) | async-done | bytes 786448 | tf_op jit(solution)/shard_map/psum | solution.py:148
  283.4 1.7 multiply_reduce_fusion
  285.1 1.7 multiply_convert_fusion
  286.8 6.9 %fusion.6 = f32[16,2,1024]{2,0,1:T(8,128)S(1)} fusion(bf16[6144,1024]{1,0:T(8,128)(2,1)} %param.25, bf16[16,2,6144]{2,1,0:T(2,128)(2,1)S(1)} %multiply_convert_fusion), kind=kOutput, calls=%fused_computation.6 | convolution fusion | flops 402653184 | bytes 13107200 | tf_op jit(solution)/shard_map/pmd,dc->pmc/dot_general | solution.py:49
  293.7 12.6 %fusion.2 = f32[16,2,6144]{2,0,1:T(8,128)S(1)} fusion(bf16[1024,6144]{1,0:T(8,128)(2,1)} %param.27, bf16[6144,1024]{1,0:T(8,128)(2,1)} %param.26, bf16[16,2,6144]{2,1,0:T(2,128)(2,1)S(1)} %multiply_convert_fusion, f32[16,2,1024]{2,0,1:T(8,128)S(1)} %fusion.6), kind=kOutput, calls=%fused_computation.2 | convolution fusion | flops 805502976 | bytes 26476544 | tf_op jit(solution)/shard_map/pmc,cd->pmd/dot_general | solution.py:64
  306.3 1.5 copy.58
  308.5 91.2 %all-reduce.6.cloned.1.call-done = f32[16,2,6144]{2,1,0:T(2,128)} async-done(((f32[16,2,6144]{2,1,0:T(2,128)}), f32[16,2,6144]{2,1,0:T(2,128)}) %all-reduce.6.cloned.1.call-update) | async-done | bytes 786448
  399.7 2.1 fusion.62
  (82 shorter events, 12.8 us)
Async XLA Ops:
  6.5 1.1 copy-start
  6.5 39.6 %copy-start.5 = (s32[2]{0:T(128)S(1)}, s32[2]{0:T(128)}, u32[]{:S(2)}) copy-start(s32[2]{0:T(128)} %param.15) | copy-start | bytes 28
  34.0 116.8 %copy-start.3 = (f32[6144]{0:T(1024)S(1)}, f32[6144]{0:T(1024)}, u32[]{:S(2)}) copy-start(f32[6144]{0:T(1024)} %param.20) | copy-start | bytes 73732
  42.2 10.5 %all-to-all-start = ((bf16[16,2,1152]{2,1,0:T(2,128)(2,1)}), bf16[16,2,1152]{2,1,0:T(2,128)(2,1)S(1)}, u32[]{:S(2)}, u32[]{:S(2)}) async-start(bf16[16,2,1152]{2,1,0:T(2,128)(2,1)} %copy.49), calls=%async_computation | async-start | bytes 147456 | tf_op jit(solution)/shard_map/all_to_all | solution.py:59
  45.7 236.2 %all-reduce.4.cloned.1.call-start = ((), (), s32[]{:S(2)}) async-start(), calls=%async_computation.2 | async-start | bytes 1572864 | tf_op jit(solution)/shard_map/psum | solution.py:148
  53.0 23.6 %collective-permute-start = (bf16[1,2,6144]{2,1,0:T(2,128)(2,1)S(1)}, bf16[1,2,6144]{2,1,0:T(2,128)(2,1)S(1)}, u32[]{:S(2)}, u32[]{:S(2)}) collective-permute-start(bf16[1,2,6144]{2,1,0:T(2,128)(2,1)S(1)} %get-tuple-element.7), channel_id=1, source_target_pairs={{0,1},{1,2},{2,3},{3,4},{4,5},{5,6},{6,7},{7,8},{8,9},{9,10},{10,1... | collective-permute-start | bytes 73736 | tf_op jit(solution)/shard_map/ppermute | solution.py:25
  53.0 24.0 %collective-permute-start.1 = (bf16[1,2,6144]{2,1,0:T(2,128)(2,1)S(1)}, bf16[1,2,6144]{2,1,0:T(2,128)(2,1)S(1)}, u32[]{:S(2)}, u32[]{:S(2)}) collective-permute-start(bf16[1,2,6144]{2,1,0:T(2,128)(2,1)S(1)} %get-tuple-element.7), channel_id=1, source_target_pairs={{0,15},{1,0},{2,1},{3,2},{4,3},{5,4},{6,5},{7,6},{8,7},{9,8},{10,9... | collective-permute-start | bytes 73736 | tf_op jit(solution)/shard_map/ppermute | solution.py:30
  76.6 6.0 %collective-permute-start.2 = (bf16[1,2,6144]{2,1,0:T(2,128)(2,1)S(1)}, bf16[1,2,6144]{2,1,0:T(2,128)(2,1)S(1)}, u32[]{:S(2)}, u32[]{:S(2)}) collective-permute-start(bf16[1,2,6144]{2,1,0:T(2,128)(2,1)S(1)} %collective-permute-done), channel_id=1, source_target_pairs={{0,1},{1,2},{2,3},{3,4},{4,5},{5,6},{6,7},{7,8},{8,9},{9,10},{10,1... | collective-permute-start | bytes 73736 | tf_op jit(solution)/shard_map/ppermute | solution.py:25
  77.0 5.6 %collective-permute-start.3 = (bf16[1,2,6144]{2,1,0:T(2,128)(2,1)S(1)}, bf16[1,2,6144]{2,1,0:T(2,128)(2,1)S(1)}, u32[]{:S(2)}, u32[]{:S(2)}) collective-permute-start(bf16[1,2,6144]{2,1,0:T(2,128)(2,1)S(1)} %collective-permute-done.1), channel_id=1, source_target_pairs={{0,15},{1,0},{2,1},{3,2},{4,3},{5,4},{6,5},{7,6},{8,7},{9,8},{10,9... | collective-permute-start | bytes 73736 | tf_op jit(solution)/shard_map/ppermute | solution.py:30
  82.6 5.9 %collective-permute-start.4 = (bf16[1,2,6144]{2,1,0:T(2,128)(2,1)S(1)}, bf16[1,2,6144]{2,1,0:T(2,128)(2,1)S(1)}, u32[]{:S(2)}, u32[]{:S(2)}) collective-permute-start(bf16[1,2,6144]{2,1,0:T(2,128)(2,1)S(1)} %collective-permute-done.2), channel_id=1, source_target_pairs={{0,1},{1,2},{2,3},{3,4},{4,5},{5,6},{6,7},{7,8},{8,9},{9,10},{10,1... | collective-permute-start | bytes 73736 | tf_op jit(solution)/shard_map/ppermute | solution.py:25
  82.6 5.9 %collective-permute-start.5 = (bf16[1,2,6144]{2,1,0:T(2,128)(2,1)S(1)}, bf16[1,2,6144]{2,1,0:T(2,128)(2,1)S(1)}, u32[]{:S(2)}, u32[]{:S(2)}) collective-permute-start(bf16[1,2,6144]{2,1,0:T(2,128)(2,1)S(1)} %collective-permute-done.3), channel_id=1, source_target_pairs={{0,15},{1,0},{2,1},{3,2},{4,3},{5,4},{6,5},{7,6},{8,7},{9,8},{10,9... | collective-permute-start | bytes 73736 | tf_op jit(solution)/shard_map/ppermute | solution.py:30
  88.5 5.9 %collective-permute-start.6 = (bf16[1,2,6144]{2,1,0:T(2,128)(2,1)S(1)}, bf16[1,2,6144]{2,1,0:T(2,128)(2,1)S(1)}, u32[]{:S(2)}, u32[]{:S(2)}) collective-permute-start(bf16[1,2,6144]{2,1,0:T(2,128)(2,1)S(1)} %collective-permute-done.4), channel_id=1, source_target_pairs={{0,1},{1,2},{2,3},{3,4},{4,5},{5,6},{6,7},{7,8},{8,9},{9,10},{10,1... | collective-permute-start | bytes 73736 | tf_op jit(solution)/shard_map/ppermute | solution.py:25
  88.6 5.9 %collective-permute-start.7 = (bf16[1,2,6144]{2,1,0:T(2,128)(2,1)S(1)}, bf16[1,2,6144]{2,1,0:T(2,128)(2,1)S(1)}, u32[]{:S(2)}, u32[]{:S(2)}) collective-permute-start(bf16[1,2,6144]{2,1,0:T(2,128)(2,1)S(1)} %collective-permute-done.5), channel_id=1, source_target_pairs={{0,15},{1,0},{2,1},{3,2},{4,3},{5,4},{6,5},{7,6},{8,7},{9,8},{10,9... | collective-permute-start | bytes 73736 | tf_op jit(solution)/shard_map/ppermute | solution.py:30
  94.5 5.9 %collective-permute-start.8 = (bf16[1,2,6144]{2,1,0:T(2,128)(2,1)S(1)}, bf16[1,2,6144]{2,1,0:T(2,128)(2,1)S(1)}, u32[]{:S(2)}, u32[]{:S(2)}) collective-permute-start(bf16[1,2,6144]{2,1,0:T(2,128)(2,1)S(1)} %collective-permute-done.6), channel_id=1, source_target_pairs={{0,1},{1,2},{2,3},{3,4},{4,5},{5,6},{6,7},{7,8},{8,9},{9,10},{10,1... | collective-permute-start | bytes 73736 | tf_op jit(solution)/shard_map/ppermute | solution.py:25
  94.5 5.9 %collective-permute-start.9 = (bf16[1,2,6144]{2,1,0:T(2,128)(2,1)S(1)}, bf16[1,2,6144]{2,1,0:T(2,128)(2,1)S(1)}, u32[]{:S(2)}, u32[]{:S(2)}) collective-permute-start(bf16[1,2,6144]{2,1,0:T(2,128)(2,1)S(1)} %collective-permute-done.7), channel_id=1, source_target_pairs={{0,15},{1,0},{2,1},{3,2},{4,3},{5,4},{6,5},{7,6},{8,7},{9,8},{10,9... | collective-permute-start | bytes 73736 | tf_op jit(solution)/shard_map/ppermute | solution.py:30
  100.4 5.9 %collective-permute-start.10 = (bf16[1,2,6144]{2,1,0:T(2,128)(2,1)S(1)}, bf16[1,2,6144]{2,1,0:T(2,128)(2,1)S(1)}, u32[]{:S(2)}, u32[]{:S(2)}) collective-permute-start(bf16[1,2,6144]{2,1,0:T(2,128)(2,1)S(1)} %collective-permute-done.8), channel_id=1, source_target_pairs={{0,1},{1,2},{2,3},{3,4},{4,5},{5,6},{6,7},{7,8},{8,9},{9,10},{10,1... | collective-permute-start | bytes 73736 | tf_op jit(solution)/shard_map/ppermute | solution.py:25
  100.5 5.9 %collective-permute-start.11 = (bf16[1,2,6144]{2,1,0:T(2,128)(2,1)S(1)}, bf16[1,2,6144]{2,1,0:T(2,128)(2,1)S(1)}, u32[]{:S(2)}, u32[]{:S(2)}) collective-permute-start(bf16[1,2,6144]{2,1,0:T(2,128)(2,1)S(1)} %collective-permute-done.9), channel_id=1, source_target_pairs={{0,15},{1,0},{2,1},{3,2},{4,3},{5,4},{6,5},{7,6},{8,7},{9,8},{10,9... | collective-permute-start | bytes 73736 | tf_op jit(solution)/shard_map/ppermute | solution.py:30
  106.4 5.9 %collective-permute-start.12 = (bf16[1,2,6144]{2,1,0:T(2,128)(2,1)S(1)}, bf16[1,2,6144]{2,1,0:T(2,128)(2,1)S(1)}, u32[]{:S(2)}, u32[]{:S(2)}) collective-permute-start(bf16[1,2,6144]{2,1,0:T(2,128)(2,1)S(1)} %collective-permute-done.10), channel_id=1, source_target_pairs={{0,1},{1,2},{2,3},{3,4},{4,5},{5,6},{6,7},{7,8},{8,9},{9,10},{10,1... | collective-permute-start | bytes 73736 | tf_op jit(solution)/shard_map/ppermute | solution.py:25
  106.4 6.0 %collective-permute-start.13 = (bf16[1,2,6144]{2,1,0:T(2,128)(2,1)S(1)}, bf16[1,2,6144]{2,1,0:T(2,128)(2,1)S(1)}, u32[]{:S(2)}, u32[]{:S(2)}) collective-permute-start(bf16[1,2,6144]{2,1,0:T(2,128)(2,1)S(1)} %collective-permute-done.11), channel_id=1, source_target_pairs={{0,15},{1,0},{2,1},{3,2},{4,3},{5,4},{6,5},{7,6},{8,7},{9,8},{10,9... | collective-permute-start | bytes 73736 | tf_op jit(solution)/shard_map/ppermute | solution.py:30
  112.3 5.9 %collective-permute-start.14 = (bf16[1,2,6144]{2,1,0:T(2,128)(2,1)S(1)}, bf16[1,2,6144]{2,1,0:T(2,128)(2,1)S(1)}, u32[]{:S(2)}, u32[]{:S(2)}) collective-permute-start(bf16[1,2,6144]{2,1,0:T(2,128)(2,1)S(1)} %collective-permute-done.12), channel_id=1, source_target_pairs={{0,1},{1,2},{2,3},{3,4},{4,5},{5,6},{6,7},{7,8},{8,9},{9,10},{10,1... | collective-permute-start | bytes 73736 | tf_op jit(solution)/shard_map/ppermute | solution.py:25
  176.6 108.5 %copy-start.4 = (f32[6144]{0:T(1024)S(1)}, f32[6144]{0:T(1024)}, u32[]{:S(2)}) copy-start(f32[6144]{0:T(1024)} %param.24) | copy-start | bytes 73732
  189.9 0.9 copy-start.2
  190.8 208.9 %all-reduce.6.cloned.1.call-start = ((), (), s32[]{:S(2)}) async-start(), calls=%async_computation.3 | async-start | bytes 1572864
  286.7 115.0 %copy-start.1 = (bf16[64,6144]{1,0:T(8,128)(2,1)S(1)}, bf16[64,6144]{1,0:T(8,128)(2,1)}, u32[]{:S(2)}) copy-start(bf16[64,6144]{1,0:T(8,128)(2,1)} %param.16) | copy-start | bytes 2359300
  293.7 14.2 %copy-start.6 = (u32[32]{0:T(128)S(1)}, u32[32]{0:T(128)}, u32[]{:S(2)}) copy-start(u32[32]{0:T(128)} %constant.130) | copy-start | bytes 388
Sparse Core Ops, SparseCore 0:
  190.9 90.9 all-reduce.3
  307.9 91.7 all-reduce.5
